TPU v7x, 256 devices: a whole 4x4x8 slice. The times are simulated.
256 devices in a mesh: island: 16 (over y_hi, z), inner: 16 (over y_lo, x, core).
Axes of the slice: x: 4, y: 4 (y_hi: 2, y_lo: 2; y = y_hi * 2 + y_lo), z: 8, core: 2. Of those that a mesh axis runs over, the one named last changes fastest.
Arguments:
- island_delta: float32 [16, 2, 8192, 512], P('island', None, 'inner'), may hold values from -200 to 200, as said below
- params: float32 [2, 8192, 512], P(None, 'inner'), may hold values from -6 to 6
- momentum: float32 [2, 8192, 512], P(None, 'inner'), may hold values from -6 to 6
Outputs:
- new_params: float32 [2, 8192, 512], P(None, 'inner')
- new_momentum: float32 [2, 8192, 512], P(None, 'inner')
Inputs may be any that keep to these rules, and one draw needn't show every extreme that they name: `island_delta`: entries are finite and of mixed sign.
All inputs are finite; a program needn't handle non-finite values.
Results may differ from a plain program's by a relative error of at most 0.0003.
Values sent between devices are 32-bit elements; how exact they have to be, the bound alone decides.
A program may use at most 64 MiB of HBM per device.

v0:
```python
import jax
import jax.numpy as jnp
from jax import lax
from jax.sharding import PartitionSpec as P

D = 8192
HEAD = 128
KVH = 4


def outer_update(average, params, momentum, mean_square):
    factor = jnp.minimum(jnp.float32(1.0), 0.5 / jnp.sqrt(mean_square + 1e-06))
    clipped = factor * average
    new_momentum = 0.9 * momentum + clipped
    new_params = params - 0.7 * (clipped + 0.9 * new_momentum)
    return (new_params, new_momentum)


def body(island_delta, params, momentum):
    replicas = lax.axis_size("island")
    count = 2 * D * KVH * HEAD
    own_delta = island_delta[0]
    part = lax.psum_scatter(own_delta, "island", scatter_dimension=1, tiled=True) / replicas
    part_sq = jnp.sum(part * part)
    average = lax.all_gather(part, "island", axis=1, tiled=True)
    total_sq = lax.psum(part_sq, ("island", "inner"))
    return outer_update(average, params, momentum, total_sq / count)


def solution(mesh):
    in_specs = (P("island", None, "inner", None), P(None, "inner", None), P(None, "inner", None))
    out_specs = (P(None, "inner", None), P(None, "inner", None))
    return jax.shard_map(body, mesh=mesh, in_specs=in_specs, out_specs=out_specs, check_vma=False)
```

profile of v0, /device:TPU:4, one launch (start us, length us, event | category | flops | bytes accessed | tf_op | source)
XLA Modules:
  0.0 319.3 jit_solution(10462347991436961005)
XLA Ops:
  7.2 0.0 copy-start
  7.2 0.0 reduce-scatter.2.cloned.1.call-start
  7.2 0.7 reduce-scatter.2.cloned.1.call-update
  7.9 0.0 all-gather.2.cloned.1.call-start
  8.0 212.8 %reduce-scatter.2.cloned.1.call-done = f32[2,32,512]{2,1,0:T(8,128)} async-done(((f32[2,512,512]{2,1,0:T(8,128)}), f32[2,32,512]{2,1,0:T(8,128)}) %reduce-scatter.2.cloned.1.call-update) | async-done | bytes 131088 | tf_op jit(solution)/shard_map/reduce_scatter | solution.py:23
  220.7 2.2 multiply_reduce_fusion
  222.9 0.0 all-gather.2.cloned.1.call-update
  222.9 74.1 %psum.7 = f32[]{:T(128)} all-reduce(f32[]{:T(128)} %get-tuple-element.4), channel_id=1, replica_groups=mesh['island'=16,'inner'=16] {'island','inner'}, use_global_device_ids=true, to_apply=%region_2.0 | all-reduce | flops 1 | bytes 8 | tf_op jit(solution)/shard_map/psum | solution.py:26
  297.7 9.6 %all-gather.2.cloned.1.call-done = f32[2,512,512]{2,1,0:T(8,128)} async-done(((f32[2,32,512]{2,1,0:T(8,128)}), f32[2,512,512]{2,1,0:T(8,128)}) %all-gather.2.cloned.1.call-update) | async-done | bytes 2097168 | tf_op jit(solution)/shard_map/all_gather | solution.py:25
  307.4 0.0 copy-done
  307.4 5.0 %multiply_subtract_fusion = (f32[2,512,512]{2,1,0:T(8,128)}, f32[2,512,512]{2,1,0:T(8,128)}) fusion(f32[2,512,512]{2,1,0:T(8,128)S(1)} %copy-done, f32[2,512,512]{2,1,0:T(8,128)} %all-gather.2.cloned.1.call-done, f32[]{:T(128)S(6)} %min_shard_map.3, f32[2,512,512]{2,1,0:T(8,128)} %param.5), kind=kLoop, calls=%fused_computation | loop fusion | flops 3670016 | bytes 10485764 | tf_op jit(solution)/shard_map/sub | solution.py:15
Async XLA Ops:
  7.2 300.2 %copy-start = (f32[2,512,512]{2,1,0:T(8,128)S(1)}, f32[2,512,512]{2,1,0:T(8,128)}, u32[]{:S(2)}) copy-start(f32[2,512,512]{2,1,0:T(8,128)} %param.4) | copy-start | bytes 6291460
  7.2 213.6 %reduce-scatter.2.cloned.1.call-start = ((), (), s32[]{:S(2)}) async-start(), calls=%async_computation.1 | async-start | bytes 2228224 | tf_op jit(solution)/shard_map/reduce_scatter | solution.py:23
  7.9 299.5 %all-gather.2.cloned.1.call-start = ((), (), s32[]{:S(2)}) async-start(), calls=%async_computation.2 | async-start | bytes 2228224 | tf_op jit(solution)/shard_map/all_gather | solution.py:25
Sparse Core Ops, SparseCore 0:
  11.9 208.8 reduce-scatter.1
  223.9 83.4 all-gather.1
where the time goes:
time: 320 us; the launch traced here: 319 us
  waiting for transfers between devices  223 us (70%)
  blocking collectives  74.1 us (23%)
  between operations  14.7 us (5%)
  other arithmetic  7.19 us (2%)
    reduce_scatter x1, waiting for transfers between devices, body(): lax.psum_scatter(own_delta, 'island', scatter_dimension=1, tiled=True)  213 us
    psum x1, blocking collectives, body(): total_sq = lax.psum(part_sq, ('island', 'inner'))  74.1 us
    all_gather x1, waiting for transfers between devices, body(): average = lax.all_gather(part, 'island', axis=1, tiled=True)  9.64 us
  transfers between devices with their start and end apart: 2, of which 2 were waited for; matrix products, arithmetic and copies ran while one was open for 0% of the time, Pallas kernels for 0%

commit v1 on v0

--- a/solution.py
+++ b/solution.py
@@ -22,7 +22,17 @@
     own_delta = island_delta[0]
     part = lax.psum_scatter(own_delta, "island", scatter_dimension=1, tiled=True) / replicas
     part_sq = jnp.sum(part * part)
-    average = lax.all_gather(part, "island", axis=1, tiled=True)
+
+    def wait_samples(local_array):
+        wide_out = lax.all_to_all(
+            jnp.stack([local_array for _ in range(lax.axis_size("island"))]),
+            split_axis=0,
+            concat_axis=0,
+            axis_name="island",
+        )
+        return jnp.concatenate(wide_out, axis=1)
+
+    average = wait_samples(part)
     total_sq = lax.psum(part_sq, ("island", "inner"))
     return outer_update(average, params, momentum, total_sq / count)
 

time: 320 us -> 331 us (1.034)
  blocking collectives: 74.1 us -> 87.7 us
  waiting for transfers between devices: 223 us -> 214 us
  starting transfers between devices: 0.08 us -> 5.55 us
  local copies, waits for them, and re-layouts: 0.01 us -> 3.53 us
    psum x1, blocking collectives: 74.1 us -> 87.7 us  [body(): total_sq = lax.psum(part_sq, ('island', 'inner'))]
    all_gather x1 -> x0, waiting for transfers between devices: 9.64 us -> none  [body(): average = lax.all_gather(part, 'island', axis=1, tiled=True)]
    all_to_all x0 -> x1, starting transfers between devices: none -> 5.52 us  [wait_samples(): lax.all_to_all(jnp.stack([local_array for _ in range(lax.axis_size('islan...]
  transfers between devices with their start and end apart: 2 -> 2, of which waited for: 2 -> 1; matrix products, arithmetic and copies ran while one was open for 0% -> 0% of each run, Pallas kernels for 0% -> 0%
where the time goes in v1:
time: 331 us; the launch traced here: 330 us
  waiting for transfers between devices  214 us (65%)
  blocking collectives  87.7 us (26%)
  between operations  14.8 us (4%)
  starting transfers between devices  5.55 us (2%)
  other arithmetic  4.58 us (1%)
  local copies, waits for them, and re-layouts  3.53 us (1%)
    reduce_scatter x1, waiting for transfers between devices, body(): lax.psum_scatter(own_delta, 'island', scatter_dimension=1, tiled=True)  213 us
    psum x1, blocking collectives, body(): total_sq = lax.psum(part_sq, ('island', 'inner'))  87.7 us
  transfers between devices with their start and end apart: 2, of which 1 were waited for; matrix products, arithmetic and copies ran while one was open for 0% of the time, Pallas kernels for 0%

profile of v1, /device:TPU:4, one launch (start us, length us, event | category | flops | bytes accessed | tf_op | source)
XLA Modules:
  0.0 329.6 jit_solution(13972475714461157551)
XLA Ops:
  7.2 0.0 reduce-scatter.2.cloned.1.call-start
  7.2 0.7 reduce-scatter.2.cloned.1.call-update
  7.9 212.8 %reduce-scatter.2.cloned.1.call-done = f32[2,32,512]{2,1,0:T(8,128)} async-done(((f32[2,512,512]{2,1,0:T(8,128)}), f32[2,32,512]{2,1,0:T(8,128)}) %reduce-scatter.2.cloned.1.call-update) | async-done | bytes 131088 | tf_op jit(solution)/shard_map/reduce_scatter | solution.py:23
  220.7 1.5 multiply_reduce_fusion
  222.3 1.6 stack.2
  223.9 5.5 %all-to-all-start = ((f32[16,2,32,512]{3,2,1,0:T(8,128)}), f32[16,2,32,512]{3,2,1,0:T(8,128)S(1)}, u32[]{:S(2)}, u32[]{:S(2)}) async-start(f32[16,2,32,512]{3,2,1,0:T(8,128)} %stack.2), calls=%async_computation.1 | async-start | bytes 4194304 | tf_op jit(solution)/shard_map/all_to_all | solution.py:27
  229.4 87.7 %psum.7 = f32[]{:T(128)} all-reduce(f32[]{:T(128)} %get-tuple-element.4), channel_id=1, replica_groups=mesh['island'=16,'inner'=16] {'island','inner'}, use_global_device_ids=true, to_apply=%region_2.0 | all-reduce | flops 1 | bytes 8 | tf_op jit(solution)/shard_map/psum | solution.py:36
  317.7 0.0 all-to-all-done
  317.8 0.0 copy-start
  317.8 0.0 copy-start.1
  317.8 0.2 copy_multiply_fusion
  318.0 1.3 copy-done
  319.4 0.6 copy-done.1
  320.0 2.8 fusion.1
Async XLA Ops:
  7.2 213.6 %reduce-scatter.2.cloned.1.call-start = ((), (), s32[]{:S(2)}) async-start(), calls=%async_computation.2 | async-start | bytes 2228224 | tf_op jit(solution)/shard_map/reduce_scatter | solution.py:23
  223.9 93.9 %all-to-all-start = ((f32[16,2,32,512]{3,2,1,0:T(8,128)}), f32[16,2,32,512]{3,2,1,0:T(8,128)S(1)}, u32[]{:S(2)}, u32[]{:S(2)}) async-start(f32[16,2,32,512]{3,2,1,0:T(8,128)} %stack.2), calls=%async_computation.1 | async-start | bytes 4194304 | tf_op jit(solution)/shard_map/all_to_all | solution.py:27
  317.8 1.6 copy-start
  317.8 2.2 copy-start.1
Sparse Core Ops, SparseCore 0:
  11.9 208.8 reduce-scatter.1
